TPU v7x, 32 devices: a whole 2x2x4 slice. The times are simulated.
32 devices in a mesh: shard: 4 (over y, x), context: 8 (over z, core).
Axes of the slice: x: 2, y: 2, z: 4, core: 2. Of those that a mesh axis runs over, the one named last changes fastest.
Arguments:
- tokens: bfloat16 [4096, 1536], P(('shard', 'context')), may hold values from -6 to 6
- segments: int32 [4096], P(('shard', 'context')), may hold values from 0 to 3, as said below
- positions: int32 [4096], P(('shard', 'context')), may hold values from 0 to 1022, as said below
- attn_gain: float32 [1536], replicated, may hold values from 0.5 to 1.5
- w_qkv: bfloat16 [1536, 2048], P('shard'), may hold values from -0.15625 to 0.15625
- b_qkv: float32 [2048], replicated, may hold values from -3 to 3
- w_out: bfloat16 [1536, 1536], P('shard'), may hold values from -0.625 to 0.625
- ffn_gain: float32 [1536], replicated, may hold values from 0.5 to 1.5
- w_gate_up: bfloat16 [1536, 2, 8960], P('shard', None, 'context'), may hold values from -0.15625 to 0.15625
- w_down: bfloat16 [8960, 1536], P('context', 'shard'), may hold values from -0.1875 to 0.1875
- cotangent: bfloat16 [4096, 1536], P(('shard', 'context')), may hold values from -6 to 6
Outputs:
- output: float32 [4096, 1536], P(('shard', 'context'))
- grad_tokens: float32 [4096, 1536], P(('shard', 'context'))
- grad_attn_gain: float32 [1536], P(('shard', 'context'))
- grad_w_qkv: float32 [1536, 2048], P(('shard', 'context'))
- grad_b_qkv: float32 [2048], P(('shard', 'context'))
- grad_w_out: float32 [1536, 1536], P(('shard', 'context'))
- grad_ffn_gain: float32 [1536], P(('shard', 'context'))
- grad_w_gate_up: float32 [1536, 2, 8960], P('shard', None, 'context')
- grad_w_down: float32 [8960, 1536], P('context', 'shard')
Inputs may be any that keep to these rules, and one draw needn't show every extreme that they name: `segments`: segment numbers start at 0 in every sequence, never fall along it (a number may be skipped), and the last token of every sequence has 3. `positions`: a token's position is its index minus the index of the first token of its segment.
All inputs are finite; a program needn't handle non-finite values.
Results may differ from a plain program's by a relative error of at most 0.015.
Values may be sent and summed in bfloat16 or wider, within the bound.
No kernel may reach another device: no remote copies, remote signals or barrier semaphores. Data moves between devices by JAX's collectives and lax.ppermute only.
A program may use at most 192 MiB of HBM per device.

v0:
```python
import jax
import jax.numpy as jnp
from jax import lax
from jax.sharding import PartitionSpec as P

D = 1536
HEADS_Q = 12
HEADS_KV = 2
HEAD_DIM = 128
EPS = 1e-06
THETA = 1000000.0
NEG = -1e30


def shifted(block, axis, distance):
    devices = range(lax.axis_size(axis))
    route = [((i - distance) % len(devices), i) for i in devices]
    return lax.ppermute(block, axis, route)


def rope_tables(positions, head_size):
    half = head_size // 2
    frequency = THETA ** (-(jnp.arange(half, dtype=jnp.float32) * (2.0 / head_size)))
    angle = positions.astype(jnp.float32)[:, None] * frequency[None, :]
    cosine = jnp.cos(angle)
    sine_part = jnp.sin(angle)
    return (jnp.concatenate([cosine, cosine], 1), jnp.concatenate([sine_part, sine_part], 1))


def rotate(values, cosine, sine_part):
    half = values.shape[-1] // 2
    turned = jnp.concatenate([-values[..., half:], values[..., :half]], -1)
    return values * cosine[:, None, :] + turned * sine_part[:, None, :]


def unrotate(grads, cosine, sine_part):
    half = grads.shape[-1] // 2
    scaled = grads * sine_part[:, None, :]
    return grads * cosine[:, None, :] + jnp.concatenate(
        [scaled[..., half:], -scaled[..., :half]], -1
    )


def norm_back(values, inverse, weighted):
    return inverse * weighted - values * inverse**3 * jnp.mean(
        weighted * values, axis=-1, keepdims=True
    )


def block_scores(query, piece, start, query_index, query_seg, scale):
    keys, values, key_seg = piece
    key_index = start + jnp.arange(keys.shape[0], dtype=jnp.int32)
    scores = jnp.einsum("bhgd,jhd->hgbj", query, keys, preferred_element_type=jnp.float32) * scale
    allowed = (key_index[None, :] <= query_index[:, None]) & (
        key_seg[None, :] == query_seg[:, None]
    )
    return (jnp.where(allowed[None, None], scores, NEG), allowed)


def stats_update(carry, piece, start, query, query_index, query_seg, scale):
    best, total = carry
    scores, allowed = block_scores(query, piece, start, query_index, query_seg, scale)
    new_best = jnp.maximum(best, jnp.max(scores, axis=-1))
    factor = jnp.exp(best - new_best)
    weights = jnp.where(allowed[None, None], jnp.exp(scores - new_best[..., None]), 0.0)
    return (new_best, total * factor + jnp.sum(weights, axis=-1))


def attend_update(accum, piece, start, query, lse, query_index, query_seg, scale):
    scores, allowed = block_scores(query, piece, start, query_index, query_seg, scale)
    probs = jnp.where(allowed[None, None], jnp.exp(scores - lse[..., None]), 0.0).astype(
        jnp.bfloat16
    )
    return accum + jnp.einsum("hgbj,jhd->hgbd", probs, piece[1], preferred_element_type=jnp.float32)


def backward_update(piece, start, query, grad_grouped, lse, delta, query_index, query_seg, scale):
    keys, values, key_seg = piece
    scores, allowed = block_scores(query, piece, start, query_index, query_seg, scale)
    probs = jnp.where(allowed[None, None], jnp.exp(scores - lse[..., None]), 0.0)
    grad_values = jnp.einsum(
        "hgbj,bhgd->jhd",
        probs.astype(jnp.bfloat16),
        grad_grouped,
        preferred_element_type=jnp.float32,
    )
    grad_probs = jnp.einsum(
        "bhgd,jhd->hgbj", grad_grouped, values, preferred_element_type=jnp.float32
    )
    grad_scores = (probs * (grad_probs - delta[..., None])).astype(jnp.bfloat16)
    grad_query = (
        jnp.einsum("hgbj,jhd->bhgd", grad_scores, keys, preferred_element_type=jnp.float32) * scale
    )
    grad_keys = (
        jnp.einsum("hgbj,bhgd->jhd", grad_scores, query, preferred_element_type=jnp.float32) * scale
    )
    return (grad_query, grad_keys, grad_values)


def swiglu_forward(normed, gate_up_weight, down_weight):
    units = down_weight.shape[0]
    both = jnp.dot(
        normed,
        gate_up_weight.reshape(gate_up_weight.shape[0], 2 * units),
        preferred_element_type=jnp.float32,
    )
    gate = both[:, :units]
    upper = both[:, units:]
    sigma = jax.nn.sigmoid(gate)
    activated = gate * sigma
    hidden = (activated * upper).astype(jnp.bfloat16)
    return (gate, upper, sigma, activated, hidden)


def swiglu_grads(cot_rows, down_weight, gate, upper, sigma, activated):
    grad_hidden = jnp.dot(cot_rows, down_weight.T, preferred_element_type=jnp.float32)
    grad_gate = grad_hidden * upper * sigma * (1.0 + gate * (1.0 - sigma))
    grad_upper = grad_hidden * activated
    return jnp.concatenate([grad_gate, grad_upper], 1).astype(jnp.bfloat16)


def body(
    tokens,
    segments,
    positions,
    attn_gain,
    w_qkv,
    b_qkv,
    w_out,
    ffn_gain,
    w_gate_up,
    w_down,
    cotangent,
):
    rows = tokens.shape[0]
    group = HEADS_Q // HEADS_KV
    q_width = HEADS_Q * HEAD_DIM
    kv_width = HEADS_KV * HEAD_DIM
    scale = HEAD_DIM ** (-0.5)
    length = lax.axis_size("context")
    place = lax.axis_index("context")
    query_index = place * rows + jnp.arange(rows, dtype=jnp.int32)
    query_seg = segments.astype(jnp.bfloat16)
    qkv_full, out_full = (
        lax.all_gather(w_qkv, "shard", axis=0, tiled=True),
        lax.all_gather(w_out, "shard", axis=0, tiled=True),
    )
    tokens_wide = tokens.astype(jnp.float32)
    inverse_one = lax.rsqrt(jnp.mean(tokens_wide * tokens_wide, axis=-1, keepdims=True) + EPS)
    normed_one = (tokens_wide * inverse_one * attn_gain).astype(jnp.bfloat16)
    projected = jnp.dot(normed_one, qkv_full, preferred_element_type=jnp.float32) + b_qkv
    cosine, sine_part = rope_tables(positions, HEAD_DIM)
    query = rotate(
        projected[:, :q_width].reshape(rows, HEADS_Q, HEAD_DIM), cosine, sine_part
    ).astype(jnp.bfloat16)
    keys = rotate(
        projected[:, q_width : q_width + kv_width].reshape(rows, HEADS_KV, HEAD_DIM),
        cosine,
        sine_part,
    ).astype(jnp.bfloat16)
    values = (
        projected[:, q_width + kv_width :].reshape(rows, HEADS_KV, HEAD_DIM).astype(jnp.bfloat16)
    )
    grouped = query.reshape(rows, HEADS_KV, group, HEAD_DIM)
    own = (keys, values, query_seg)

    def cycle_pass(update, init):

        def pass_step(step, state):
            carry, held = state
            source = (place + step) % length
            carry = update(carry, held, source * rows)
            held = shifted((held[0], held[1], held[2]), "context", -1)
            return (carry, held)

        return lax.fori_loop(0, length, pass_step, (init, own))[0]

    stats_init = (
        jnp.full((HEADS_KV, group, rows), NEG, jnp.float32),
        jnp.zeros((HEADS_KV, group, rows), jnp.float32),
    )
    best, total = cycle_pass(
        lambda carry, piece, start: stats_update(
            carry, piece, start, grouped, query_index, query_seg, scale
        ),
        stats_init,
    )
    lse = best + jnp.log(total)
    accum = cycle_pass(
        lambda carry, piece, start: attend_update(
            carry, piece, start, grouped, lse, query_index, query_seg, scale
        ),
        jnp.zeros((HEADS_KV, group, rows, HEAD_DIM), jnp.float32),
    )
    attended = jnp.transpose(accum, (2, 0, 1, 3)).reshape(rows, q_width).astype(jnp.bfloat16)
    mixed = tokens_wide + jnp.dot(attended, out_full, preferred_element_type=jnp.float32)
    inverse_two = lax.rsqrt(jnp.mean(mixed * mixed, axis=-1, keepdims=True) + EPS)
    normed_two = (mixed * inverse_two * ffn_gain).astype(jnp.bfloat16)
    gate_up_part, down_part = (
        lax.all_gather(w_gate_up, "shard", axis=0, tiled=True),
        lax.all_gather(w_down, "shard", axis=1, tiled=True),
    )
    normed_all, cot_all = (
        lax.all_gather(normed_two, "context", axis=0, tiled=True),
        lax.all_gather(cotangent, "context", axis=0, tiled=True),
    )
    gate, upper, sigma, activated, hidden = swiglu_forward(normed_all, gate_up_part, down_part)
    down_rows = lax.psum_scatter(
        jnp.dot(hidden, down_part, preferred_element_type=jnp.float32).astype(jnp.bfloat16),
        "context",
        scatter_dimension=0,
        tiled=True,
    ).astype(jnp.float32)
    output = mixed + down_rows
    down_grad_part = jnp.dot(hidden.T, cot_all, preferred_element_type=jnp.float32)
    grad_both = swiglu_grads(cot_all, down_part, gate, upper, sigma, activated)
    units = down_part.shape[0]
    gate_up_grad_part = jnp.dot(
        normed_all.T, grad_both, preferred_element_type=jnp.float32
    ).reshape(D, 2, units)
    gate_up_flat = gate_up_part.reshape(D, 2 * units)
    grad_normed_two = lax.psum_scatter(
        jnp.dot(grad_both, gate_up_flat.T, preferred_element_type=jnp.float32),
        "context",
        scatter_dimension=0,
        tiled=True,
    )
    grad_gate_up, grad_down = (
        lax.psum_scatter(
            gate_up_grad_part.astype(jnp.bfloat16), "shard", scatter_dimension=0, tiled=True
        ).astype(jnp.float32),
        lax.psum_scatter(
            down_grad_part.astype(jnp.bfloat16), "shard", scatter_dimension=1, tiled=True
        ).astype(jnp.float32),
    )
    gain_two_term = jnp.sum(grad_normed_two * mixed * inverse_two, axis=0)
    grad_mixed = cotangent.astype(jnp.float32) + norm_back(
        mixed, inverse_two, grad_normed_two * ffn_gain
    )
    grad_mixed_low = grad_mixed.astype(jnp.bfloat16)
    out_term = jnp.dot(attended.T, grad_mixed_low, preferred_element_type=jnp.float32)
    grad_attended = jnp.dot(grad_mixed_low, out_full.T, preferred_element_type=jnp.float32).astype(
        jnp.bfloat16
    )
    grad_grouped = grad_attended.reshape(rows, HEADS_KV, group, HEAD_DIM)
    attended_grouped = attended.reshape(rows, HEADS_KV, group, HEAD_DIM)
    delta = jnp.transpose(
        jnp.sum(grad_grouped.astype(jnp.float32) * attended_grouped.astype(jnp.float32), axis=-1),
        (1, 2, 0),
    )
    zero_query = jnp.zeros((rows, HEADS_KV, group, HEAD_DIM), jnp.float32)
    zero_keys = jnp.zeros((rows, HEADS_KV, HEAD_DIM), jnp.float32)

    def back_step(step, state):
        grad_query, held, carried = state
        source = (place + step) % length
        part_query, part_keys, part_values = backward_update(
            held, source * rows, grouped, grad_grouped, lse, delta, query_index, query_seg, scale
        )
        carried = (carried[0] + part_keys, carried[1] + part_values)
        held = shifted((held[0], held[1], held[2]), "context", -1)
        carried = (
            shifted(carried[0].astype(jnp.bfloat16), "context", -1).astype(jnp.float32),
            shifted(carried[1].astype(jnp.bfloat16), "context", -1).astype(jnp.float32),
        )
        return (grad_query + part_query, held, carried)

    grad_query, _, (grad_keys, grad_values) = lax.fori_loop(
        0, length, back_step, (zero_query, own, (zero_keys, zero_keys))
    )
    grad_q = unrotate(grad_query.reshape(rows, HEADS_Q, HEAD_DIM), cosine, sine_part).reshape(
        rows, q_width
    )
    grad_k = unrotate(grad_keys, cosine, sine_part).reshape(rows, kv_width)
    grad_projected = jnp.concatenate([grad_q, grad_k, grad_values.reshape(rows, kv_width)], 1)
    bias_term = jnp.sum(grad_projected, axis=0)
    grad_projected_low = grad_projected.astype(jnp.bfloat16)
    qkv_term = jnp.dot(normed_one.T, grad_projected_low, preferred_element_type=jnp.float32)
    grad_normed_one = jnp.dot(grad_projected_low, qkv_full.T, preferred_element_type=jnp.float32)
    gain_one_term = jnp.sum(grad_normed_one * tokens_wide * inverse_one, axis=0)
    grad_tokens = grad_mixed + norm_back(tokens_wide, inverse_one, grad_normed_one * attn_gain)
    summed = (
        lax.psum_scatter(gain_one_term, ("shard", "context"), scatter_dimension=0, tiled=True),
        lax.psum_scatter(qkv_term, ("shard", "context"), scatter_dimension=0, tiled=True),
        lax.psum_scatter(bias_term, ("shard", "context"), scatter_dimension=0, tiled=True),
        lax.psum_scatter(out_term, ("shard", "context"), scatter_dimension=0, tiled=True),
        lax.psum_scatter(gain_two_term, ("shard", "context"), scatter_dimension=0, tiled=True),
    )
    return (
        output,
        grad_tokens,
        summed[0],
        summed[1],
        summed[2],
        summed[3],
        summed[4],
        grad_gate_up,
        grad_down,
    )


def solution(mesh):
    return jax.shard_map(
        body,
        mesh=mesh,
        in_specs=(
            P(("shard", "context"), None),
            P(("shard", "context")),
            P(("shard", "context")),
            P(),
            P("shard", None),
            P(),
            P("shard", None),
            P(),
            P("shard", None, "context"),
            P("context", "shard"),
            P(("shard", "context"), None),
        ),
        out_specs=(
            P(("shard", "context"), None),
            P(("shard", "context"), None),
            P(("shard", "context")),
            P(("shard", "context"), None),
            P(("shard", "context")),
            P(("shard", "context"), None),
            P(("shard", "context")),
            P("shard", None, "context"),
            P("context", "shard"),
        ),
        check_vma=False,
    )
```

profile of v0, /device:TPU:0, one launch (start us, length us, event | category | flops | bytes accessed | tf_op | source)
XLA Modules:
  0.0 918.2 jit_solution(16799553422252278018)
XLA Ops:
  13.0 69.7 %all-gather.7.cloned.1.call-done = bf16[1536,2048]{1,0:T(8,128)(2,1)} async-done(((bf16[384,2048]{1,0:T(8,128)(2,1)}), bf16[1536,2048]{1,0:T(8,128)(2,1)}) %all-gather.7.cloned.1.call-update) | async-done | bytes 6291472 | tf_op jit(solution)/shard_map/all_gather | solution.py:145
  82.7 3.8 convolution_add_fusion.2
  87.7 44.2 %while.70 = (s32[]{:T(128)}, f32[2,6,128]{2,1,0:T(8,128)S(1)}, f32[2,6,128]{2,1,0:T(8,128)S(1)}, bf16[128,2,128]{2,0,1:T(8,128)(2,1)S(1)}, bf16[128]{0:T(256)(12...) while((s32[]{:T(128)}, f32[2,6,128]{2,1,0:T(8,128)S(1)}, ...), condition=%wide.region_4.5_spmd.clone, body=%wide.region_1.4_spmd.clone.sunk | while | flops 51601168 | bytes 2558317 | solution.py:176
  98.0 3.7 collective-permute-start
  103.6 3.7 collective-permute-start
  109.3 3.7 collective-permute-start
  114.9 3.7 collective-permute-start
  120.6 3.7 collective-permute-start
  126.2 3.7 collective-permute-start
  132.4 50.7 %while.71 = (s32[]{:T(128)}, f32[2,6,128,128]{3,2,1,0:T(8,128)S(1)}, bf16[128,2,128]{2,0,1:T(8,128)(2,1)S(1)}, bf16[128,2,128]{2,0,1:T(8,128)(2,1)S(1)}, bf16[12...) while((s32[]{:T(128)}, ...), condition=%wide.region_6.7_spmd.clone, body=%wide.region_5.6_spmd.clone.sunk | while | flops 102121744 | bytes 2927004 | solution.py:176
  132.5 3.7 collective-permute-start.2
  138.7 3.8 collective-permute-start.2
  145.1 3.8 collective-permute-start.2
  151.4 3.8 collective-permute-start.2
  157.8 3.8 collective-permute-start.2
  164.1 3.8 collective-permute-start.2
  170.5 3.8 collective-permute-start.2
  176.8 3.8 collective-permute-start.2
  183.4 3.6 multiply_reduce_fusion.3
  190.1 28.0 %all-gather.13.cloned.1.call-done = bf16[1536,2,1120]{0,2,1:T(8,128)(2,1)} async-done(((bf16[384,2,1120]{0,2,1:T(8,128)(2,1)}), bf16[1536,2,1120]{0,2,1:T(8,128)(2,1)}) %all-gather.13.cloned.1.call-update) | async-done | bytes 6881296 | tf_op jit(solution)/shard_map/all_gather | solution.py:200
  218.1 40.3 %all-gather.11.cloned.1.call-done = bf16[1024,1536]{1,0:T(8,128)(2,1)} async-done(((bf16[128,1536]{1,0:T(8,128)(2,1)}), bf16[1024,1536]{1,0:T(8,128)(2,1)}) %all-gather.11.cloned.1.call-update) | async-done | bytes 3145744 | tf_op jit(solution)/shard_map/all_gather | solution.py:204
  258.4 12.6 %fusion.79 = f32[1024,2240]{0,1:T(8,128)} fusion(bf16[1024,1536]{1,0:T(8,128)(2,1)} %all-gather.11.cloned.1.call-done, bf16[1536,2240]{0,1:T(8,128)(2,1)} %bitcast.218), kind=kOutput, calls=%fused_computation.141 | convolution fusion | flops 7046430720 | bytes 19202048 | tf_op jit(solution)/shard_map/dot_general | solution.py:102
  271.1 34.1 %all-gather.15.cloned.1.call-done = bf16[1120,1536]{1,0:T(8,128)(2,1)} async-done(((bf16[1120,384]{1,0:T(8,128)(2,1)}), bf16[1120,1536]{1,0:T(8,128)(2,1)}) %all-gather.15.cloned.1.call-update) | async-done | bytes 3440656 | tf_op jit(solution)/shard_map/all_gather | solution.py:201
  305.2 39.7 %all-gather.17.cloned.1.call-done = bf16[1024,1536]{1,0:T(8,128)(2,1)} async-done(((bf16[128,1536]{1,0:T(8,128)(2,1)}), bf16[1024,1536]{1,0:T(8,128)(2,1)}) %all-gather.17.cloned.1.call-update) | async-done | bytes 3145744 | tf_op jit(solution)/shard_map/all_gather | solution.py:205
  345.0 12.4 %multiply_convert_fusion.1 = (bf16[1024,1120]{0,1:T(8,128)(2,1)S(1)}, bf16[1024,1120]{0,1:T(8,128)(2,1)S(1)}, bf16[1024,1120]{0,1:T(8,128)(2,1)}) fusion(f32[1024,2240]{0,1:T(8,128)} %fusion.79, bf16[1024,1536]{1,0:T(8,128)(2,1)} %all-gather.17.cloned.1.call-done, bf16[1120,1536]{1,0:T(8,128)(2,1)} %all-gather.15.cloned.1.call-done), kind=kOutput, calls=%fused_computation.67 | convolution fusion | flops 3540418560 | bytes 22642688 | tf_op jit(solution)/shard_map/dot_general | solution.py:116
  359.5 9.6 %fusion.48 = f32[1024,1536]{1,0:T(8,128)} fusion(bf16[1536,2240]{0,1:T(8,128)(2,1)S(1)} %bitcast.219, bf16[1024,1120]{0,1:T(8,128)(2,1)S(1)} %get-tuple-element.1096, bf16[1024,1120]{0,1:T(8,128)(2,1)S(1)} %get-tuple-element.1095), kind=kOutput, calls=%fused_computation.72 | convolution fusion | flops 7055605760 | bytes 17760256 | tf_op jit(solution)/shard_map/dot_general | solution.py:223
  369.3 8.7 convolution_convert_fusion.2
  378.0 8.1 convolution_convert_fusion.1
  386.1 5.7 copy.89
  391.8 12.2 %convolution_convert_fusion = bf16[1536,2240]{0,1:T(8,128)(2,1)} fusion(bf16[1024,1536]{1,0:T(8,128)(2,1)} %all-gather.11.cloned.1.call-done, bf16[1024,1120]{0,1:T(8,128)(2,1)} %copy-done.19, bf16[1024,1120]{0,1:T(8,128)(2,1)} %copy-done.18), kind=kOutput, calls=%fused_computation.63 | convolution fusion | flops 7059046400 | bytes 14614528 | tf_op jit(solution)/shard_map/dot_general | solution.py:218
  404.0 9.9 %copy.92 = bf16[1536,2240]{1,0:T(8,128)(2,1)} copy(bf16[1536,2240]{0,1:T(8,128)(2,1)} %convolution_convert_fusion) | data formatting | bytes 13762560
  415.4 22.4 %reduce-scatter.13.cloned.1.call-done = f32[128,1536]{1,0:T(8,128)} async-done(((f32[1024,1536]{1,0:T(8,128)}), f32[128,1536]{1,0:T(8,128)}) %reduce-scatter.13.cloned.1.call-update) | async-done | bytes 786448 | tf_op jit(solution)/shard_map/reduce_scatter | solution.py:222
  440.3 38.7 %reduce-scatter.11.cloned.1.call-done = bf16[128,1536]{1,0:T(8,128)(2,1)} async-done(((bf16[1024,1536]{1,0:T(8,128)(2,1)}), bf16[128,1536]{1,0:T(8,128)(2,1)}) %reduce-scatter.11.cloned.1.call-update) | async-done | bytes 393232 | tf_op jit(solution)/shard_map/reduce_scatter | solution.py:208
  481.6 4.0 convolution_convert_fusion.3
  489.0 5.0 fusion.62
  494.0 90.0 %while.72 = (s32[]{:T(128)}, f32[128,2,6,128]{3,0,2,1:T(8,128)S(1)}, bf16[128,2,128]{2,0,1:T(8,128)(2,1)S(1)}, bf16[128,2,128]{2,0,1:T(8,128)(2,1)S(1)}, bf16[12...) while((s32[]{:T(128)}, ...), condition=%wide.region_13.14_spmd.clone, body=%wide.region_12.13_spmd.clone.sunk | while | flops 254198032 | bytes 9028110 | solution.py:268
  502.0 3.7 collective-permute-start.5
  515.1 3.6 collective-permute-start.5
  525.1 3.7 collective-permute-start.5
  537.8 3.6 collective-permute-start.5
  547.9 3.6 collective-permute-start.5
  560.9 3.6 collective-permute-start.5
  571.0 3.6 collective-permute-start.5
  585.8 6.4 fusion.67
  596.3 5.2 fusion.57
  601.5 39.4 %all-reduce.3 = (f32[1536]{0:T(1024)S(1)}, f32[2048]{0:T(1024)S(1)}, f32[1536]{0:T(1024)S(1)}) all-reduce(f32[1536]{0:T(1024)S(1)} %get-tuple-element.1022, f32[2048]{0:T(1024)S(1)} %fusion.60, f32[1536]{0:T(1024)S(1)} %copy-done.10), channel_id=4, replica_groups=mesh['shard'=4,'context'=8] {'shard','context'}, use_global_device_ids=true, to_apply=%region_16.17.clone | all-reduce | flops 5120 | bytes 40960
  648.7 102.1 %reduce-scatter.17.cloned.1.call-done = f32[48,1536]{1,0:T(8,128)} async-done(((f32[1536,1536]{1,0:T(8,128)}), f32[48,1536]{1,0:T(8,128)}) %reduce-scatter.17.cloned.1.call-update) | async-done | bytes 294928 | tf_op jit(solution)/shard_map/reduce_scatter | solution.py:286
  750.8 160.3 %reduce-scatter.15.cloned.1.call-done = f32[48,2048]{1,0:T(8,128)} async-done(((f32[1536,2048]{1,0:T(8,128)}), f32[48,2048]{1,0:T(8,128)}) %reduce-scatter.15.cloned.1.call-update) | async-done | bytes 393232 | tf_op jit(solution)/shard_map/reduce_scatter | solution.py:284
  (507 shorter events, 142.1 us)
Async XLA Ops:
  7.2 75.4 %all-gather.7.cloned.1.call-start = ((), (), s32[]{:S(2)}) async-start(), calls=%async_computation.6 | async-start | bytes 7864320 | tf_op jit(solution)/shard_map/all_gather | solution.py:145
  8.0 175.5 %all-gather.9.cloned.1.call-start = ((), (), s32[]{:S(2)}) async-start(), calls=%async_computation.7 | async-start | bytes 5898240 | tf_op jit(solution)/shard_map/all_gather | solution.py:146
  8.7 209.4 %all-gather.13.cloned.1.call-start = ((), (), s32[]{:S(2)}) async-start(), calls=%async_computation.9 | async-start | bytes 8601600 | tf_op jit(solution)/shard_map/all_gather | solution.py:200
  9.4 249.0 %all-gather.11.cloned.1.call-start = ((), (), s32[]{:S(2)}) async-start(), calls=%async_computation.8 | async-start | bytes 3538944 | tf_op jit(solution)/shard_map/all_gather | solution.py:204
  92.5 5.5 collective-permute-start
  98.0 5.6 collective-permute-start
  103.6 5.6 collective-permute-start
  109.3 5.6 collective-permute-start
  114.9 5.6 collective-permute-start
  120.6 5.6 collective-permute-start
  126.2 5.6 collective-permute-start
  132.5 6.3 collective-permute-start.2
  138.7 6.3 collective-permute-start.2
  145.1 6.3 collective-permute-start.2
  151.4 6.3 collective-permute-start.2
  157.8 6.3 collective-permute-start.2
  164.1 6.3 collective-permute-start.2
  170.5 6.3 collective-permute-start.2
  176.8 6.3 collective-permute-start.2
  188.4 116.8 %all-gather.15.cloned.1.call-start = ((), (), s32[]{:S(2)}) async-start(), calls=%async_computation.10 | async-start | bytes 4300800 | tf_op jit(solution)/shard_map/all_gather | solution.py:201
  189.0 155.9 %all-gather.17.cloned.1.call-start = ((), (), s32[]{:S(2)}) async-start(), calls=%async_computation.12 | async-start | bytes 3538944 | tf_op jit(solution)/shard_map/all_gather | solution.py:205
  189.6 248.2 %reduce-scatter.13.cloned.1.call-start = ((), (), s32[]{:S(2)}) async-start(), calls=%async_computation.13 | async-start | bytes 7077888 | tf_op jit(solution)/shard_map/reduce_scatter | solution.py:222
  369.0 109.9 %reduce-scatter.11.cloned.1.call-start = ((), (), s32[]{:S(2)}) async-start(), calls=%async_computation.11 | async-start | bytes 3538944 | tf_op jit(solution)/shard_map/reduce_scatter | solution.py:208
  377.9 214.4 %reduce-scatter.21.cloned.1.call-start = ((), (), s32[]{:S(2)}) async-start(), calls=%async_computation.17 | async-start | bytes 4423680
  391.7 252.1 %reduce-scatter.19.cloned.1.call-start = ((), (), s32[]{:S(2)}) async-start(), calls=%async_computation.16 | async-start | bytes 8847360
  413.9 336.9 %reduce-scatter.17.cloned.1.call-start = ((), (), s32[]{:S(2)}) async-start(), calls=%async_computation.15 | async-start | bytes 9732096 | tf_op jit(solution)/shard_map/reduce_scatter | solution.py:286
  493.9 417.2 %reduce-scatter.15.cloned.1.call-start = ((), (), s32[]{:S(2)}) async-start(), calls=%async_computation.14 | async-start | bytes 12976128 | tf_op jit(solution)/shard_map/reduce_scatter | solution.py:284
  494.0 7.9 collective-permute-start.5
  495.7 6.3 collective-permute-start.6
  502.0 13.1 %collective-permute-start.5 = (bf16[128,2,128]{2,0,1:T(8,128)(2,1)S(1)}, bf16[128,2,128]{2,0,1:T(8,128)(2,1)S(1)}, u32[]{:S(2)}, u32[]{:S(2)}) collective-permute-start(bf16[128,2,128]{2,0,1:T(8,128)(2,1)S(1)} %copy.135), channel_id=1, source_target_pairs={{1,0},{2,1},{3,2},{4,3},{5,4},{6,5},{7,6},{0,7},{9,8},{10,9},{11,1... | collective-permute-start | bytes 196616 | tf_op jit(solution)/shard_map/while/body/eval_jaxpr/ppermute | solution.py:18
  505.7 9.4 %collective-permute-start.6 = (bf16[128,2,128]{2,0,1:T(8,128)(2,1)S(1)}, bf16[128,2,128]{2,0,1:T(8,128)(2,1)S(1)}, u32[]{:S(2)}, u32[]{:S(2)}) collective-permute-start(bf16[128,2,128]{2,0,1:T(8,128)(2,1)S(1)} %copy.136), channel_id=1, source_target_pairs={{1,0},{2,1},{3,2},{4,3},{5,4},{6,5},{7,6},{0,7},{9,8},{10,9},{11,1... | collective-permute-start | bytes 196616 | tf_op jit(solution)/shard_map/while/body/eval_jaxpr/ppermute | solution.py:18
  507.0 8.1 collective-permute-start.7
  515.1 9.9 %collective-permute-start.5 = (bf16[128,2,128]{2,0,1:T(8,128)(2,1)S(1)}, bf16[128,2,128]{2,0,1:T(8,128)(2,1)S(1)}, u32[]{:S(2)}, u32[]{:S(2)}) collective-permute-start(bf16[128,2,128]{2,0,1:T(8,128)(2,1)S(1)} %copy.135), channel_id=1, source_target_pairs={{1,0},{2,1},{3,2},{4,3},{5,4},{6,5},{7,6},{0,7},{9,8},{10,9},{11,1... | collective-permute-start | bytes 196616 | tf_op jit(solution)/shard_map/while/body/eval_jaxpr/ppermute | solution.py:18
  518.8 6.3 collective-permute-start.6
  525.1 12.7 %collective-permute-start.5 = (bf16[128,2,128]{2,0,1:T(8,128)(2,1)S(1)}, bf16[128,2,128]{2,0,1:T(8,128)(2,1)S(1)}, u32[]{:S(2)}, u32[]{:S(2)}) collective-permute-start(bf16[128,2,128]{2,0,1:T(8,128)(2,1)S(1)} %copy.135), channel_id=1, source_target_pairs={{1,0},{2,1},{3,2},{4,3},{5,4},{6,5},{7,6},{0,7},{9,8},{10,9},{11,1... | collective-permute-start | bytes 196616 | tf_op jit(solution)/shard_map/while/body/eval_jaxpr/ppermute | solution.py:18
  528.8 9.0 collective-permute-start.6
  530.1 7.7 collective-permute-start.7
  537.8 10.0 %collective-permute-start.5 = (bf16[128,2,128]{2,0,1:T(8,128)(2,1)S(1)}, bf16[128,2,128]{2,0,1:T(8,128)(2,1)S(1)}, u32[]{:S(2)}, u32[]{:S(2)}) collective-permute-start(bf16[128,2,128]{2,0,1:T(8,128)(2,1)S(1)} %copy.135), channel_id=1, source_target_pairs={{1,0},{2,1},{3,2},{4,3},{5,4},{6,5},{7,6},{0,7},{9,8},{10,9},{11,1... | collective-permute-start | bytes 196616 | tf_op jit(solution)/shard_map/while/body/eval_jaxpr/ppermute | solution.py:18
  541.5 6.4 collective-permute-start.6
  547.9 13.0 %collective-permute-start.5 = (bf16[128,2,128]{2,0,1:T(8,128)(2,1)S(1)}, bf16[128,2,128]{2,0,1:T(8,128)(2,1)S(1)}, u32[]{:S(2)}, u32[]{:S(2)}) collective-permute-start(bf16[128,2,128]{2,0,1:T(8,128)(2,1)S(1)} %copy.135), channel_id=1, source_target_pairs={{1,0},{2,1},{3,2},{4,3},{5,4},{6,5},{7,6},{0,7},{9,8},{10,9},{11,1... | collective-permute-start | bytes 196616 | tf_op jit(solution)/shard_map/while/body/eval_jaxpr/ppermute | solution.py:18
  551.5 9.4 %collective-permute-start.6 = (bf16[128,2,128]{2,0,1:T(8,128)(2,1)S(1)}, bf16[128,2,128]{2,0,1:T(8,128)(2,1)S(1)}, u32[]{:S(2)}, u32[]{:S(2)}) collective-permute-start(bf16[128,2,128]{2,0,1:T(8,128)(2,1)S(1)} %copy.136), channel_id=1, source_target_pairs={{1,0},{2,1},{3,2},{4,3},{5,4},{6,5},{7,6},{0,7},{9,8},{10,9},{11,1... | collective-permute-start | bytes 196616 | tf_op jit(solution)/shard_map/while/body/eval_jaxpr/ppermute | solution.py:18
  552.8 8.1 collective-permute-start.7
  560.9 10.0 %collective-permute-start.5 = (bf16[128,2,128]{2,0,1:T(8,128)(2,1)S(1)}, bf16[128,2,128]{2,0,1:T(8,128)(2,1)S(1)}, u32[]{:S(2)}, u32[]{:S(2)}) collective-permute-start(bf16[128,2,128]{2,0,1:T(8,128)(2,1)S(1)} %copy.135), channel_id=1, source_target_pairs={{1,0},{2,1},{3,2},{4,3},{5,4},{6,5},{7,6},{0,7},{9,8},{10,9},{11,1... | collective-permute-start | bytes 196616 | tf_op jit(solution)/shard_map/while/body/eval_jaxpr/ppermute | solution.py:18
  564.6 6.4 collective-permute-start.6
  565.8 5.1 collective-permute-start.7
  571.0 13.0 %collective-permute-start.5 = (bf16[128,2,128]{2,0,1:T(8,128)(2,1)S(1)}, bf16[128,2,128]{2,0,1:T(8,128)(2,1)S(1)}, u32[]{:S(2)}, u32[]{:S(2)}) collective-permute-start(bf16[128,2,128]{2,0,1:T(8,128)(2,1)S(1)} %copy.135), channel_id=1, source_target_pairs={{1,0},{2,1},{3,2},{4,3},{5,4},{6,5},{7,6},{0,7},{9,8},{10,9},{11,1... | collective-permute-start | bytes 196616 | tf_op jit(solution)/shard_map/while/body/eval_jaxpr/ppermute | solution.py:18
  574.6 9.4 %collective-permute-start.6 = (bf16[128,2,128]{2,0,1:T(8,128)(2,1)S(1)}, bf16[128,2,128]{2,0,1:T(8,128)(2,1)S(1)}, u32[]{:S(2)}, u32[]{:S(2)}) collective-permute-start(bf16[128,2,128]{2,0,1:T(8,128)(2,1)S(1)} %copy.136), channel_id=1, source_target_pairs={{1,0},{2,1},{3,2},{4,3},{5,4},{6,5},{7,6},{0,7},{9,8},{10,9},{11,1... | collective-permute-start | bytes 196616 | tf_op jit(solution)/shard_map/while/body/eval_jaxpr/ppermute | solution.py:18
  575.9 8.1 collective-permute-start.7
  (64 other events, 977.8 us)
Sparse Core Ops, SparseCore 0:
  9.9 72.7 all-gather.6
  84.5 56.9 all-gather.8
  143.3 74.7 all-gather.12
  220.2 38.2 all-gather.10
  260.1 45.0 all-gather.14
  306.7 38.2 all-gather.16
  369.2 68.6 reduce-scatter.12
  440.1 38.8 reduce-scatter.10
  482.1 46.4 reduce-scatter.20
  531.5 76.5 reduce-scatter.18
  614.5 136.2 reduce-scatter.16
  757.3 153.7 reduce-scatter.14
where the time goes:
time: 924 us; the launch traced here: 918 us
  waiting for transfers between devices  557 us (60%)
  matrix products  122 us (13%)
  starting transfers between devices  105 us (11%)
  local copies, waits for them, and re-layouts  40.6 us (4%)
  blocking collectives  39.4 us (4%)
  other arithmetic  36.7 us (4%)
  between operations  14.9 us (2%)
    reduce_scatter x1, waiting for transfers between devices, body(): lax.psum_scatter(qkv_term, ('shard', 'context'), scatter_dimension=0, til...  160 us
    ppermute x80, starting transfers between devices, shifted(): return lax.ppermute(block, axis, route)  104 us
    reduce_scatter x1, waiting for transfers between devices, body(): lax.psum_scatter(out_term, ('shard', 'context'), scatter_dimension=0, til...  102 us
    all_gather x1, waiting for transfers between devices, body(): lax.all_gather(w_qkv, 'shard', axis=0, tiled=True)  69.7 us
    all_gather x1, waiting for transfers between devices, body(): lax.all_gather(normed_two, 'context', axis=0, tiled=True)  40.3 us
    all_gather x1, waiting for transfers between devices, body(): lax.all_gather(cotangent, 'context', axis=0, tiled=True)  39.7 us
    unnamed x1, blocking collectives  39.4 us
    reduce_scatter x1, waiting for transfers between devices, body(): lax.psum_scatter(jnp.dot(hidden, down_part, preferred_element_type=jnp.fl...  38.7 us
  transfers between devices with their start and end apart: 92, of which 36 were waited for; matrix products, arithmetic and copies ran while one was open for 19% of the time, Pallas kernels for 0%

commit v1 on v0

--- a/solution.py
+++ b/solution.py
@@ -1,3 +1,4 @@
+import functools
 import jax
 import jax.numpy as jnp
 from jax import lax
@@ -10,6 +11,37 @@
 EPS = 1e-06
 THETA = 1000000.0
 NEG = -1e30
+
+
+def wrap_the_state(array_in, row_axis):
+    all_values = lax.axis_size(row_axis)
+    placed = lax.axis_index(row_axis)
+    field_out, block_out, outcome_arr = (all_values, placed, array_in.shape[0])
+    side_arr = jnp.zeros(
+        [w * field_out if c == 0 else w for c, w in enumerate(array_in.shape)], array_in.dtype
+    )
+    block_now = lax.dynamic_update_slice_in_dim(side_arr, array_in, block_out * outcome_arr, axis=0)
+    seen_now = extra = array_in
+    dev_i = 1
+    while dev_i < field_out // 2 + 1:
+        seen_now = lax.ppermute(
+            seen_now, row_axis, [(c, (c + 1) % field_out) for c in range(field_out)]
+        )
+        block_now = lax.dynamic_update_slice_in_dim(
+            block_now, seen_now, (block_out - dev_i) % field_out * outcome_arr, axis=0
+        )
+        if 2 * dev_i < field_out:
+            extra = lax.ppermute(
+                extra, row_axis, [(c, (c - 1) % field_out) for c in range(field_out)]
+            )
+            block_now = lax.dynamic_update_slice_in_dim(
+                block_now, extra, (block_out + dev_i) % field_out * outcome_arr, axis=0
+            )
+        dev_i = dev_i + 1
+    return block_now
+
+
+pair_goods = functools.partial(wrap_the_state, row_axis="context")
 
 
 def shifted(block, axis, distance):
@@ -201,7 +233,7 @@
         lax.all_gather(w_down, "shard", axis=1, tiled=True),
     )
     normed_all, cot_all = (
-        lax.all_gather(normed_two, "context", axis=0, tiled=True),
+        pair_goods(normed_two),
         lax.all_gather(cotangent, "context", axis=0, tiled=True),
     )
     gate, upper, sigma, activated, hidden = swiglu_forward(normed_all, gate_up_part, down_part)

time: 924 us -> 886 us (0.959)
  waiting for transfers between devices: 557 us -> 500 us
  starting transfers between devices: 105 us -> 116 us
    all_gather x1 -> x0, waiting for transfers between devices: 40.3 us -> none  [body(): lax.all_gather(normed_two, 'context', axis=0, tiled=True)]
    ppermute x0 -> x7, waiting for transfers between devices: none -> 29.8 us  [the longest x4 29.8 us: wrap_the_state(): lax.ppermute(seen_now, row_axis, [(c, (c + 1) % field_out) for c in range...]
    all_gather x1, waiting for transfers between devices: 28 us -> 0.01 us  [body(): lax.all_gather(w_gate_up, 'shard', axis=0, tiled=True)]
    all_gather x1, waiting for transfers between devices: 34.1 us -> 16.9 us  [body(): lax.all_gather(w_down, 'shard', axis=1, tiled=True)]
    ppermute x0 -> x7, starting transfers between devices: none -> 11.3 us  [the longest x3 9.45 us: wrap_the_state(): lax.ppermute(extra, row_axis, [(c, (c - 1) % field_out) for c in range(fi...]
    unnamed x57 -> x78, local copies, waits for them, and re-layouts: 28.8 us -> 32.2 us
  transfers between devices with their start and end apart: 92 -> 98, of which waited for: 36 -> 38; matrix products, arithmetic and copies ran while one was open for 19% -> 20% of each run, Pallas kernels for 0% -> 0%
where the time goes in v1:
time: 886 us; the launch traced here: 879 us
  waiting for transfers between devices  500 us (56%)
  matrix products  123 us (14%)
  starting transfers between devices  116 us (13%)
  local copies, waits for them, and re-layouts  49 us (6%)
  blocking collectives  39.2 us (4%)
  other arithmetic  35.5 us (4%)
  between operations  14.7 us (2%)
    reduce_scatter x1, waiting for transfers between devices, body(): lax.psum_scatter(qkv_term, ('shard', 'context'), scatter_dimension=0, til...  160 us
    ppermute x80, starting transfers between devices, shifted(): return lax.ppermute(block, axis, route)  104 us
    reduce_scatter x1, waiting for transfers between devices, body(): lax.psum_scatter(out_term, ('shard', 'context'), scatter_dimension=0, til...  102 us
    all_gather x1, waiting for transfers between devices, body(): lax.all_gather(w_qkv, 'shard', axis=0, tiled=True)  68.1 us
    all_gather x1, waiting for transfers between devices, body(): lax.all_gather(cotangent, 'context', axis=0, tiled=True)  39.7 us
    unnamed x1, blocking collectives  39.2 us
    reduce_scatter x1, waiting for transfers between devices, body(): lax.psum_scatter(jnp.dot(hidden, down_part, preferred_element_type=jnp.fl...  38.7 us
    unnamed x78, local copies, waits for them, and re-layouts  32.2 us
  transfers between devices with their start and end apart: 98, of which 38 were waited for; matrix products, arithmetic and copies ran while one was open for 20% of the time, Pallas kernels for 0%

profile of v1, /device:TPU:0, one launch (start us, length us, event | category | flops | bytes accessed | tf_op | source)
XLA Modules:
  0.0 878.8 jit_solution(9172420742360692012)
XLA Ops:
  14.6 68.1 %all-gather.6.cloned.1.call-done = bf16[1536,2048]{1,0:T(8,128)(2,1)} async-done(((bf16[384,2048]{1,0:T(8,128)(2,1)}), bf16[1536,2048]{1,0:T(8,128)(2,1)}) %all-gather.6.cloned.1.call-update) | async-done | bytes 6291472 | tf_op jit(solution)/shard_map/all_gather | solution.py:177
  82.7 3.8 convolution_add_fusion.2
  87.9 44.2 %while.70 = (s32[]{:T(128)}, f32[2,6,128]{2,1,0:T(8,128)S(1)}, f32[2,6,128]{2,1,0:T(8,128)S(1)}, bf16[128,2,128]{2,0,1:T(8,128)(2,1)S(1)}, bf16[128]{0:T(256)(12...) while((s32[]{:T(128)}, f32[2,6,128]{2,1,0:T(8,128)S(1)}, ...), condition=%wide.region_4.5_spmd.clone, body=%wide.region_1.4_spmd.clone.sunk | while | flops 51601168 | bytes 2558317 | solution.py:208
  98.3 3.7 collective-permute-start
  103.9 3.7 collective-permute-start
  109.6 3.7 collective-permute-start
  115.2 3.7 collective-permute-start
  120.9 3.7 collective-permute-start
  126.5 3.7 collective-permute-start
  132.7 50.7 %while.71 = (s32[]{:T(128)}, f32[2,6,128,128]{3,2,1,0:T(8,128)S(1)}, bf16[128,2,128]{2,0,1:T(8,128)(2,1)S(1)}, bf16[128,2,128]{2,0,1:T(8,128)(2,1)S(1)}, bf16[12...) while((s32[]{:T(128)}, ...), condition=%wide.region_6.7_spmd.clone, body=%wide.region_5.6_spmd.clone.sunk | while | flops 102121744 | bytes 2927004 | solution.py:208
  132.8 3.7 collective-permute-start.2
  139.0 3.8 collective-permute-start.2
  145.4 3.8 collective-permute-start.2
  151.7 3.8 collective-permute-start.2
  158.1 3.8 collective-permute-start.2
  164.4 3.8 collective-permute-start.2
  170.8 3.8 collective-permute-start.2
  177.1 3.8 collective-permute-start.2
  193.6 9.0 %collective-permute-done.10 = bf16[128,1536]{1,0:T(8,128)(2,1)S(1)} collective-permute-done((bf16[128,1536]{1,0:T(8,128)(2,1)S(1)}, bf16[128,1536]{1,0:T(8,128)(2,1)S(1)}, u32[]{:S(2)}, u32[]{:S(2)}) %collective-permute-start.10) | collective-permute-done | bytes 393248 | tf_op jit(solution)/shard_map/ppermute | solution.py:27
  207.7 7.5 collective-permute-done.12
  220.3 6.0 collective-permute-done.14
  228.3 7.4 collective-permute-done.16
  236.5 12.6 %fusion.79 = f32[1024,2240]{0,1:T(8,128)} fusion(bf16[1024,1536]{1,0:T(8,128)(2,1)} %constant_dynamic-update-slice_fusion, bf16[1536,2240]{0,1:T(8,128)(2,1)} %bitcast.218), kind=kOutput, calls=%fused_computation.149 | convolution fusion | flops 7046430720 | bytes 19202048 | tf_op jit(solution)/shard_map/dot_general | solution.py:134
  249.1 16.9 %all-gather.12.cloned.1.call-done = bf16[1120,1536]{1,0:T(8,128)(2,1)} async-done(((bf16[1120,384]{1,0:T(8,128)(2,1)}), bf16[1120,1536]{1,0:T(8,128)(2,1)}) %all-gather.12.cloned.1.call-update) | async-done | bytes 3440656 | tf_op jit(solution)/shard_map/all_gather | solution.py:233
  266.0 39.7 %all-gather.14.cloned.1.call-done = bf16[1024,1536]{1,0:T(8,128)(2,1)} async-done(((bf16[128,1536]{1,0:T(8,128)(2,1)}), bf16[1024,1536]{1,0:T(8,128)(2,1)}) %all-gather.14.cloned.1.call-update) | async-done | bytes 3145744 | tf_op jit(solution)/shard_map/all_gather | solution.py:237
  305.7 12.5 %multiply_convert_fusion.1 = (bf16[1024,1120]{0,1:T(8,128)(2,1)S(1)}, bf16[1024,1120]{0,1:T(8,128)(2,1)S(1)}, bf16[1024,1120]{0,1:T(8,128)(2,1)}) fusion(f32[1024,2240]{0,1:T(8,128)} %fusion.79, bf16[1024,1536]{1,0:T(8,128)(2,1)} %all-gather.14.cloned.1.call-done, bf16[1120,1536]{1,0:T(8,128)(2,1)} %all-gather.12.cloned.1.call-done), kind=kOutput, calls=%fused_computation.67 | convolution fusion | flops 3540418560 | bytes 22642688 | tf_op jit(solution)/shard_map/dot_general | solution.py:148
  320.3 9.6 %fusion.48 = f32[1024,1536]{1,0:T(8,128)} fusion(bf16[1536,2240]{0,1:T(8,128)(2,1)S(1)} %bitcast.219, bf16[1024,1120]{0,1:T(8,128)(2,1)S(1)} %get-tuple-element.1098, bf16[1024,1120]{0,1:T(8,128)(2,1)S(1)} %get-tuple-element.1097), kind=kOutput, calls=%fused_computation.72 | convolution fusion | flops 7055605760 | bytes 17760256 | tf_op jit(solution)/shard_map/dot_general | solution.py:255
  330.1 8.6 convolution_convert_fusion.2
  338.8 8.1 convolution_convert_fusion.1
  346.9 5.7 copy.89
  352.7 12.2 %convolution_convert_fusion = bf16[1536,2240]{0,1:T(8,128)(2,1)} fusion(bf16[1024,1536]{1,0:T(8,128)(2,1)} %constant_dynamic-update-slice_fusion, bf16[1024,1120]{0,1:T(8,128)(2,1)} %copy-done.30, bf16[1024,1120]{0,1:T(8,128)(2,1)} %copy-done.29), kind=kOutput, calls=%fused_computation.63 | convolution fusion | flops 7059046400 | bytes 14614528 | tf_op jit(solution)/shard_map/dot_general | solution.py:250
  364.9 10.3 %copy.92 = bf16[1536,2240]{1,0:T(8,128)(2,1)} copy(bf16[1536,2240]{0,1:T(8,128)(2,1)} %convolution_convert_fusion) | data formatting | bytes 13762560
  376.7 22.0 %reduce-scatter.13.cloned.1.call-done = f32[128,1536]{1,0:T(8,128)} async-done(((f32[1024,1536]{1,0:T(8,128)}), f32[128,1536]{1,0:T(8,128)}) %reduce-scatter.13.cloned.1.call-update) | async-done | bytes 786448 | tf_op jit(solution)/shard_map/reduce_scatter | solution.py:254
  401.2 38.7 %reduce-scatter.11.cloned.1.call-done = bf16[128,1536]{1,0:T(8,128)(2,1)} async-done(((bf16[1024,1536]{1,0:T(8,128)(2,1)}), bf16[128,1536]{1,0:T(8,128)(2,1)}) %reduce-scatter.11.cloned.1.call-update) | async-done | bytes 393232 | tf_op jit(solution)/shard_map/reduce_scatter | solution.py:240
  442.4 4.0 convolution_convert_fusion.3
  447.0 5.0 fusion.62
  453.0 90.5 %while.72 = (s32[]{:T(128)}, f32[128,2,6,128]{3,0,2,1:T(8,128)S(1)}, bf16[128,2,128]{2,0,1:T(8,128)(2,1)S(1)}, bf16[128,2,128]{2,0,1:T(8,128)(2,1)S(1)}, bf16[12...) while((s32[]{:T(128)}, ...), condition=%wide.region_13.14_spmd.clone, body=%wide.region_12.13_spmd.clone.sunk | while | flops 254198032 | bytes 9028110 | solution.py:300
  461.0 3.7 collective-permute-start.5
  474.2 3.6 collective-permute-start.5
  484.1 3.7 collective-permute-start.5
  497.3 3.6 collective-permute-start.5
  507.3 3.7 collective-permute-start.5
  520.4 3.6 collective-permute-start.5
  545.6 6.5 fusion.67
  557.3 5.2 fusion.57
  562.5 39.2 %all-reduce.3 = (f32[1536]{0:T(1024)S(1)}, f32[2048]{0:T(1024)S(1)}, f32[1536]{0:T(1024)S(1)}) all-reduce(f32[1536]{0:T(1024)S(1)} %get-tuple-element.1022, f32[2048]{0:T(1024)S(1)} %fusion.60, f32[1536]{0:T(1024)S(1)} %copy-done.18), channel_id=4, replica_groups=mesh['shard'=4,'context'=8] {'shard','context'}, use_global_device_ids=true, to_apply=%region_16.17.clone | all-reduce | flops 5120 | bytes 40960
  609.4 102.2 %reduce-scatter.17.cloned.1.call-done = f32[48,1536]{1,0:T(8,128)} async-done(((f32[1536,1536]{1,0:T(8,128)}), f32[48,1536]{1,0:T(8,128)}) %reduce-scatter.17.cloned.1.call-update) | async-done | bytes 294928 | tf_op jit(solution)/shard_map/reduce_scatter | solution.py:318
  711.6 160.4 %reduce-scatter.15.cloned.1.call-done = f32[48,2048]{1,0:T(8,128)} async-done(((f32[1536,2048]{1,0:T(8,128)}), f32[48,2048]{1,0:T(8,128)}) %reduce-scatter.15.cloned.1.call-update) | async-done | bytes 393232 | tf_op jit(solution)/shard_map/reduce_scatter | solution.py:316
  (547 shorter events, 167.3 us)
Async XLA Ops:
  7.2 75.4 %all-gather.6.cloned.1.call-start = ((), (), s32[]{:S(2)}) async-start(), calls=%async_computation.6 | async-start | bytes 7864320 | tf_op jit(solution)/shard_map/all_gather | solution.py:177
  8.0 175.8 %all-gather.8.cloned.1.call-start = ((), (), s32[]{:S(2)}) async-start(), calls=%async_computation.7 | async-start | bytes 5898240 | tf_op jit(solution)/shard_map/all_gather | solution.py:178
  8.7 227.7 %all-gather.10.cloned.1.call-start = ((), (), s32[]{:S(2)}) async-start(), calls=%async_computation.8 | async-start | bytes 8601600 | tf_op jit(solution)/shard_map/all_gather | solution.py:232
  9.4 256.6 %all-gather.12.cloned.1.call-start = ((), (), s32[]{:S(2)}) async-start(), calls=%async_computation.9 | async-start | bytes 4300800 | tf_op jit(solution)/shard_map/all_gather | solution.py:233
  10.0 295.7 %all-gather.14.cloned.1.call-start = ((), (), s32[]{:S(2)}) async-start(), calls=%async_computation.11 | async-start | bytes 3538944 | tf_op jit(solution)/shard_map/all_gather | solution.py:237
  10.6 388.1 %reduce-scatter.13.cloned.1.call-start = ((), (), s32[]{:S(2)}) async-start(), calls=%async_computation.12 | async-start | bytes 7077888 | tf_op jit(solution)/shard_map/reduce_scatter | solution.py:254
  98.3 5.6 collective-permute-start
  103.9 5.6 collective-permute-start
  132.8 6.3 collective-permute-start.2
  139.0 6.3 collective-permute-start.2
  145.4 6.3 collective-permute-start.2
  151.7 6.3 collective-permute-start.2
  158.1 6.3 collective-permute-start.2
  164.4 6.3 collective-permute-start.2
  170.8 6.3 collective-permute-start.2
  177.1 6.3 collective-permute-start.2
  189.8 12.7 %collective-permute-start.10 = (bf16[128,1536]{1,0:T(8,128)(2,1)S(1)}, bf16[128,1536]{1,0:T(8,128)(2,1)S(1)}, u32[]{:S(2)}, u32[]{:S(2)}) collective-permute-start(bf16[128,1536]{1,0:T(8,128)(2,1)S(1)} %get-tuple-element.1094), channel_id=1, source_target_pairs={{0,1},{1,2},{2,3},{3,4},{4,5},{5,6},{6,7},{7,0},{8,9},{9,10},{10,1... | collective-permute-start | bytes 1179656 | tf_op jit(solution)/shard_map/ppermute | solution.py:27
  191.2 11.4 %collective-permute-start.11 = (bf16[128,1536]{1,0:T(8,128)(2,1)S(1)}, bf16[128,1536]{1,0:T(8,128)(2,1)S(1)}, u32[]{:S(2)}, u32[]{:S(2)}) collective-permute-start(bf16[128,1536]{1,0:T(8,128)(2,1)S(1)} %get-tuple-element.1094), channel_id=1, source_target_pairs={{0,7},{1,0},{2,1},{3,2},{4,3},{5,4},{6,5},{7,6},{8,15},{9,8},{10,9... | collective-permute-start | bytes 1179656 | tf_op jit(solution)/shard_map/ppermute | solution.py:34
  202.5 12.6 %collective-permute-start.12 = (bf16[128,1536]{1,0:T(8,128)(2,1)S(1)}, bf16[128,1536]{1,0:T(8,128)(2,1)S(1)}, u32[]{:S(2)}, u32[]{:S(2)}) collective-permute-start(bf16[128,1536]{1,0:T(8,128)(2,1)S(1)} %collective-permute-done.10), channel_id=1, source_target_pairs={{0,1},{1,2},{2,3},{3,4},{4,5},{5,6},{6,7},{7,0},{8,9},{9,10},{10,1... | collective-permute-start | bytes 1179656 | tf_op jit(solution)/shard_map/ppermute | solution.py:27
  202.5 12.6 %collective-permute-start.13 = (bf16[128,1536]{1,0:T(8,128)(2,1)S(1)}, bf16[128,1536]{1,0:T(8,128)(2,1)S(1)}, u32[]{:S(2)}, u32[]{:S(2)}) collective-permute-start(bf16[128,1536]{1,0:T(8,128)(2,1)S(1)} %collective-permute-done.11), channel_id=1, source_target_pairs={{0,7},{1,0},{2,1},{3,2},{4,3},{5,4},{6,5},{7,6},{8,15},{9,8},{10,9... | collective-permute-start | bytes 1179656 | tf_op jit(solution)/shard_map/ppermute | solution.py:34
  215.1 11.1 %collective-permute-start.14 = (bf16[128,1536]{1,0:T(8,128)(2,1)S(1)}, bf16[128,1536]{1,0:T(8,128)(2,1)S(1)}, u32[]{:S(2)}, u32[]{:S(2)}) collective-permute-start(bf16[128,1536]{1,0:T(8,128)(2,1)S(1)} %collective-permute-done.12), channel_id=1, source_target_pairs={{0,1},{1,2},{2,3},{3,4},{4,5},{5,6},{6,7},{7,0},{8,9},{9,10},{10,1... | collective-permute-start | bytes 1179656 | tf_op jit(solution)/shard_map/ppermute | solution.py:27
  215.1 12.4 %collective-permute-start.15 = (bf16[128,1536]{1,0:T(8,128)(2,1)S(1)}, bf16[128,1536]{1,0:T(8,128)(2,1)S(1)}, u32[]{:S(2)}, u32[]{:S(2)}) collective-permute-start(bf16[128,1536]{1,0:T(8,128)(2,1)S(1)} %collective-permute-done.13), channel_id=1, source_target_pairs={{0,7},{1,0},{2,1},{3,2},{4,3},{5,4},{6,5},{7,6},{8,15},{9,8},{10,9... | collective-permute-start | bytes 1179656 | tf_op jit(solution)/shard_map/ppermute | solution.py:34
  226.2 9.4 %collective-permute-start.16 = (bf16[128,1536]{1,0:T(8,128)(2,1)S(1)}, bf16[128,1536]{1,0:T(8,128)(2,1)S(1)}, u32[]{:S(2)}, u32[]{:S(2)}) collective-permute-start(bf16[128,1536]{1,0:T(8,128)(2,1)S(1)} %collective-permute-done.14), channel_id=1, source_target_pairs={{0,1},{1,2},{2,3},{3,4},{4,5},{5,6},{6,7},{7,0},{8,9},{9,10},{10,1... | collective-permute-start | bytes 1179656 | tf_op jit(solution)/shard_map/ppermute | solution.py:27
  329.9 109.9 %reduce-scatter.11.cloned.1.call-start = ((), (), s32[]{:S(2)}) async-start(), calls=%async_computation.10 | async-start | bytes 3538944 | tf_op jit(solution)/shard_map/reduce_scatter | solution.py:240
  338.8 213.4 %reduce-scatter.21.cloned.1.call-start = ((), (), s32[]{:S(2)}) async-start(), calls=%async_computation.16 | async-start | bytes 4423680
  352.6 252.0 %reduce-scatter.19.cloned.1.call-start = ((), (), s32[]{:S(2)}) async-start(), calls=%async_computation.15 | async-start | bytes 8847360
  375.2 336.4 %reduce-scatter.17.cloned.1.call-start = ((), (), s32[]{:S(2)}) async-start(), calls=%async_computation.14 | async-start | bytes 9732096 | tf_op jit(solution)/shard_map/reduce_scatter | solution.py:318
  452.0 420.1 %reduce-scatter.15.cloned.1.call-start = ((), (), s32[]{:S(2)}) async-start(), calls=%async_computation.13 | async-start | bytes 12976128 | tf_op jit(solution)/shard_map/reduce_scatter | solution.py:316
  453.0 8.0 collective-permute-start.5
  454.7 6.3 collective-permute-start.6
  461.0 13.1 %collective-permute-start.5 = (bf16[128,2,128]{2,0,1:T(8,128)(2,1)S(1)}, bf16[128,2,128]{2,0,1:T(8,128)(2,1)S(1)}, u32[]{:S(2)}, u32[]{:S(2)}) collective-permute-start(bf16[128,2,128]{2,0,1:T(8,128)(2,1)S(1)} %copy.143), channel_id=1, source_target_pairs={{1,0},{2,1},{3,2},{4,3},{5,4},{6,5},{7,6},{0,7},{9,8},{10,9},{11,1... | collective-permute-start | bytes 196616 | tf_op jit(solution)/shard_map/while/body/eval_jaxpr/ppermute | solution.py:50
  464.8 9.4 %collective-permute-start.6 = (bf16[128,2,128]{2,0,1:T(8,128)(2,1)S(1)}, bf16[128,2,128]{2,0,1:T(8,128)(2,1)S(1)}, u32[]{:S(2)}, u32[]{:S(2)}) collective-permute-start(bf16[128,2,128]{2,0,1:T(8,128)(2,1)S(1)} %copy.144), channel_id=1, source_target_pairs={{1,0},{2,1},{3,2},{4,3},{5,4},{6,5},{7,6},{0,7},{9,8},{10,9},{11,1... | collective-permute-start | bytes 196616 | tf_op jit(solution)/shard_map/while/body/eval_jaxpr/ppermute | solution.py:50
  466.0 8.1 collective-permute-start.7
  474.2 9.9 %collective-permute-start.5 = (bf16[128,2,128]{2,0,1:T(8,128)(2,1)S(1)}, bf16[128,2,128]{2,0,1:T(8,128)(2,1)S(1)}, u32[]{:S(2)}, u32[]{:S(2)}) collective-permute-start(bf16[128,2,128]{2,0,1:T(8,128)(2,1)S(1)} %copy.143), channel_id=1, source_target_pairs={{1,0},{2,1},{3,2},{4,3},{5,4},{6,5},{7,6},{0,7},{9,8},{10,9},{11,1... | collective-permute-start | bytes 196616 | tf_op jit(solution)/shard_map/while/body/eval_jaxpr/ppermute | solution.py:50
  477.8 6.3 collective-permute-start.6
  484.1 13.1 %collective-permute-start.5 = (bf16[128,2,128]{2,0,1:T(8,128)(2,1)S(1)}, bf16[128,2,128]{2,0,1:T(8,128)(2,1)S(1)}, u32[]{:S(2)}, u32[]{:S(2)}) collective-permute-start(bf16[128,2,128]{2,0,1:T(8,128)(2,1)S(1)} %copy.143), channel_id=1, source_target_pairs={{1,0},{2,1},{3,2},{4,3},{5,4},{6,5},{7,6},{0,7},{9,8},{10,9},{11,1... | collective-permute-start | bytes 196616 | tf_op jit(solution)/shard_map/while/body/eval_jaxpr/ppermute | solution.py:50
  487.9 9.4 %collective-permute-start.6 = (bf16[128,2,128]{2,0,1:T(8,128)(2,1)S(1)}, bf16[128,2,128]{2,0,1:T(8,128)(2,1)S(1)}, u32[]{:S(2)}, u32[]{:S(2)}) collective-permute-start(bf16[128,2,128]{2,0,1:T(8,128)(2,1)S(1)} %copy.144), channel_id=1, source_target_pairs={{1,0},{2,1},{3,2},{4,3},{5,4},{6,5},{7,6},{0,7},{9,8},{10,9},{11,1... | collective-permute-start | bytes 196616 | tf_op jit(solution)/shard_map/while/body/eval_jaxpr/ppermute | solution.py:50
  489.1 8.1 collective-permute-start.7
  497.3 9.9 %collective-permute-start.5 = (bf16[128,2,128]{2,0,1:T(8,128)(2,1)S(1)}, bf16[128,2,128]{2,0,1:T(8,128)(2,1)S(1)}, u32[]{:S(2)}, u32[]{:S(2)}) collective-permute-start(bf16[128,2,128]{2,0,1:T(8,128)(2,1)S(1)} %copy.143), channel_id=1, source_target_pairs={{1,0},{2,1},{3,2},{4,3},{5,4},{6,5},{7,6},{0,7},{9,8},{10,9},{11,1... | collective-permute-start | bytes 196616 | tf_op jit(solution)/shard_map/while/body/eval_jaxpr/ppermute | solution.py:50
  500.9 6.3 collective-permute-start.6
  507.3 13.1 %collective-permute-start.5 = (bf16[128,2,128]{2,0,1:T(8,128)(2,1)S(1)}, bf16[128,2,128]{2,0,1:T(8,128)(2,1)S(1)}, u32[]{:S(2)}, u32[]{:S(2)}) collective-permute-start(bf16[128,2,128]{2,0,1:T(8,128)(2,1)S(1)} %copy.143), channel_id=1, source_target_pairs={{1,0},{2,1},{3,2},{4,3},{5,4},{6,5},{7,6},{0,7},{9,8},{10,9},{11,1... | collective-permute-start | bytes 196616 | tf_op jit(solution)/shard_map/while/body/eval_jaxpr/ppermute | solution.py:50
  511.0 9.4 %collective-permute-start.6 = (bf16[128,2,128]{2,0,1:T(8,128)(2,1)S(1)}, bf16[128,2,128]{2,0,1:T(8,128)(2,1)S(1)}, u32[]{:S(2)}, u32[]{:S(2)}) collective-permute-start(bf16[128,2,128]{2,0,1:T(8,128)(2,1)S(1)} %copy.144), channel_id=1, source_target_pairs={{1,0},{2,1},{3,2},{4,3},{5,4},{6,5},{7,6},{0,7},{9,8},{10,9},{11,1... | collective-permute-start | bytes 196616 | tf_op jit(solution)/shard_map/while/body/eval_jaxpr/ppermute | solution.py:50
  512.3 8.1 collective-permute-start.7
  520.4 10.0 %collective-permute-start.5 = (bf16[128,2,128]{2,0,1:T(8,128)(2,1)S(1)}, bf16[128,2,128]{2,0,1:T(8,128)(2,1)S(1)}, u32[]{:S(2)}, u32[]{:S(2)}) collective-permute-start(bf16[128,2,128]{2,0,1:T(8,128)(2,1)S(1)} %copy.143), channel_id=1, source_target_pairs={{1,0},{2,1},{3,2},{4,3},{5,4},{6,5},{7,6},{0,7},{9,8},{10,9},{11,1... | collective-permute-start | bytes 196616 | tf_op jit(solution)/shard_map/while/body/eval_jaxpr/ppermute | solution.py:50
  524.1 6.4 collective-permute-start.6
  530.5 13.0 %collective-permute-start.5 = (bf16[128,2,128]{2,0,1:T(8,128)(2,1)S(1)}, bf16[128,2,128]{2,0,1:T(8,128)(2,1)S(1)}, u32[]{:S(2)}, u32[]{:S(2)}) collective-permute-start(bf16[128,2,128]{2,0,1:T(8,128)(2,1)S(1)} %copy.143), channel_id=1, source_target_pairs={{1,0},{2,1},{3,2},{4,3},{5,4},{6,5},{7,6},{0,7},{9,8},{10,9},{11,1... | collective-permute-start | bytes 196616 | tf_op jit(solution)/shard_map/while/body/eval_jaxpr/ppermute | solution.py:50
  534.1 9.4 %collective-permute-start.6 = (bf16[128,2,128]{2,0,1:T(8,128)(2,1)S(1)}, bf16[128,2,128]{2,0,1:T(8,128)(2,1)S(1)}, u32[]{:S(2)}, u32[]{:S(2)}) collective-permute-start(bf16[128,2,128]{2,0,1:T(8,128)(2,1)S(1)} %copy.144), channel_id=1, source_target_pairs={{1,0},{2,1},{3,2},{4,3},{5,4},{6,5},{7,6},{0,7},{9,8},{10,9},{11,1... | collective-permute-start | bytes 196616 | tf_op jit(solution)/shard_map/while/body/eval_jaxpr/ppermute | solution.py:50
  535.4 8.1 collective-permute-start.7
  (81 other events, 1004.7 us)
Sparse Core Ops, SparseCore 0:
  9.9 72.7 all-gather.5
  84.5 56.9 all-gather.7
  143.3 74.7 all-gather.9
  219.8 46.1 all-gather.11
  267.5 38.1 all-gather.13
  330.0 68.6 reduce-scatter.12
  401.0 38.7 reduce-scatter.10
  442.9 46.4 reduce-scatter.20
  492.5 76.5 reduce-scatter.18
  575.4 136.1 reduce-scatter.16
  718.2 153.7 reduce-scatter.14
